TPU v7x, 512 devices: a whole 4x8x8 slice. The times are simulated.
512 devices in a mesh: frames: 32 (over x, y_lo, core), book: 16 (over z, y_hi).
Axes of the slice: x: 4, y: 8 (y_hi: 2, y_lo: 4; y = y_hi * 4 + y_lo), z: 8, core: 2. Of those that a mesh axis runs over, the one named last changes fastest.
Arguments:
- gate_pre: bfloat16 [8192, 6144], P('frames', 'book'), may hold values from -6 to 6
- up_pre: bfloat16 [8192, 6144], P('frames', 'book'), may hold values from -6 to 6
- down_weight: bfloat16 [6144, 4096], P('book'), may hold values from -0.109375 to 0.109375
- residual: bfloat16 [8192, 4096], P('frames', 'book'), may hold values from -6 to 6
- out_gain: bfloat16 [4096], replicated, may hold values from 0.25 to 1.75
- in_proj: bfloat16 [16, 4096, 1024], P('book', 'frames'), may hold values from -0.09375 to 0.09375
- embedding: bfloat16 [16, 1024, 1024], P('book', 'frames'), may hold values from -6 to 6
- token_ids: int32 [8192, 16], P('frames', 'book'), may hold values from 0 to 1023
- depth_gain: bfloat16 [16, 1024], P('book'), may hold values from 0.25 to 1.75
- qkv_weight: bfloat16 [16, 1024, 1536], P('book', 'frames'), may hold values from -2 to 2
Outputs:
- context: bfloat16 [8192, 16, 512], P(('frames', 'book'))
All inputs are finite; a program needn't handle non-finite values.
Results may differ from a plain program's by a relative error of at most 0.019.
Values may be sent and summed in bfloat16 or wider, within the bound.
A program may use at most 64 MiB of HBM per device.

v0:
```python
import jax
import jax.numpy as jnp
from jax import lax
from jax.sharding import Mesh
from jax.sharding import PartitionSpec as P

H = 8
HD = 64
BOOK = ("book_0", "book_1")
FRAMES_BOOK = ("frames", "book_0", "book_1")


def sum_by_axis(shard, axes, dim):
    if not axes:
        return shard
    nearer = lax.psum_scatter(shard, axes[0], scatter_dimension=dim, tiled=True)
    return sum_by_axis(nearer, axes[1:], dim)


def rms_scale(values, gain):
    moment = jnp.mean(values * values, axis=-1, keepdims=True)
    return values * lax.rsqrt(moment + 1e-05) * gain


def attend_block(grouped):
    inner = grouped[0]
    frames_here = inner.shape[0]
    books = inner.shape[1]
    width = H * HD
    queries = inner[:, :, :width].reshape(frames_here, books, H, HD)
    keys_all = inner[:, :, width : 2 * width].reshape(frames_here, books, H, HD)
    values_all = inner[:, :, 2 * width :].reshape(frames_here, books, H, HD)
    scores = jnp.einsum(
        "nkhd,njhd->nhkj", queries, keys_all, preferred_element_type=jnp.float32
    ) * HD ** (-0.5)
    causal = lax.broadcasted_iota(jnp.int32, (books, books), 0) >= lax.broadcasted_iota(
        jnp.int32, (books, books), 1
    )
    scores = jnp.where(causal, scores, -1e30)
    peak = jnp.max(scores, axis=-1, keepdims=True)
    expo = jnp.exp(scores - peak)
    probability = (expo / jnp.sum(expo, axis=-1, keepdims=True)).astype(jnp.bfloat16)
    context = jnp.einsum(
        "nhkj,njhd->nkhd", probability, values_all, preferred_element_type=jnp.float32
    )
    return context.reshape(1, frames_here, books, width).astype(jnp.bfloat16)


def gather_embedding(embedding, token_column):
    table_piece = lax.all_gather(embedding, "frames", axis=1, tiled=True)
    columns = lax.broadcasted_iota(jnp.int32, (1, table_piece.shape[1]), 1)
    matches = (token_column[:, None] == columns).astype(jnp.bfloat16)
    return jnp.dot(matches, table_piece[0], preferred_element_type=jnp.float32)


def per_device(
    gate_pre,
    up_pre,
    down_weight,
    residual,
    out_gain,
    in_proj,
    embedding,
    token_ids,
    depth_gain,
    qkv_weight,
):
    tokens_here = gate_pre.shape[0]
    book_count = lax.axis_size(BOOK)
    token_column = token_ids[:, 0]
    hidden = (jax.nn.silu(gate_pre.astype(jnp.float32)) * up_pre.astype(jnp.float32)).astype(
        jnp.bfloat16
    )
    partial_value = jnp.dot(hidden, down_weight, preferred_element_type=jnp.float32)
    share = sum_by_axis(partial_value, BOOK, 1)
    temporal = (share + residual.astype(jnp.float32)).astype(jnp.bfloat16)
    whole = lax.all_gather(temporal, BOOK, axis=1, tiled=True)
    normed = rms_scale(whole.astype(jnp.float32), out_gain.astype(jnp.float32)).astype(jnp.bfloat16)
    looked = gather_embedding(embedding, token_column)
    columns = normed
    projected = jnp.dot(
        columns,
        lax.all_gather(in_proj, "frames", axis=1, tiled=True)[0],
        preferred_element_type=jnp.float32,
    )
    depth_in = (projected + looked).astype(jnp.bfloat16)
    depth_normed = rms_scale(
        depth_in.astype(jnp.float32), depth_gain[0].astype(jnp.float32)
    ).astype(jnp.bfloat16)
    columns = depth_normed
    packed = jnp.dot(
        columns,
        lax.all_gather(qkv_weight, "frames", axis=1, tiled=True)[0],
        preferred_element_type=jnp.float32,
    ).astype(jnp.bfloat16)
    grouped = packed.reshape(book_count, tokens_here // book_count, 1, packed.shape[1])
    context = attend_block(lax.all_to_all(grouped, BOOK, split_axis=0, concat_axis=2, tiled=True))
    return context.reshape(context.shape[1], context.shape[2], context.shape[3])


def solution(mesh):
    split = Mesh(mesh.devices.reshape(mesh.shape["frames"], 8, 2), ("frames", "book_0", "book_1"))
    placed = (
        P("frames", BOOK),
        P("frames", BOOK),
        P(BOOK, None),
        P("frames", BOOK),
        P(),
        P(BOOK, "frames", None),
        P(BOOK, "frames", None),
        P("frames", BOOK),
        P(BOOK, None),
        P(BOOK, "frames", None),
    )
    return jax.shard_map(
        per_device,
        mesh=split,
        in_specs=placed,
        out_specs=P(FRAMES_BOOK, None, None),
        check_vma=False,
    )
```

profile of v0, /device:TPU:6, one launch (start us, length us, event | category | flops | bytes accessed | tf_op | source)
XLA Modules:
  0.0 469.0 jit_solution(13796978290205377564)
XLA Ops:
  6.5 0.0 copy-start
  6.5 0.0 reduce-scatter.3.cloned.1.call-start
  6.5 1.9 copy-done
  8.4 4.3 fusion.42
  12.7 0.0 copy-start.1
  12.7 0.0 copy-start.2
  12.7 0.0 copy-start.3
  12.7 0.0 reduce-scatter.3.cloned.1.call-update
  12.7 0.0 reduce-scatter.5.cloned.1.call-start
  12.8 63.5 %reduce-scatter.3.cloned.1.call-done = f32[256,512]{1,0:T(8,128)} async-done(((f32[256,4096]{1,0:T(8,128)}), f32[256,512]{1,0:T(8,128)}) %reduce-scatter.3.cloned.1.call-update) | async-done | bytes 524304 | tf_op jit(solution)/shard_map/reduce_scatter | solution.py:16
  76.2 0.0 reduce-scatter.5.cloned.1.call-update
  76.2 0.0 all-gather.5.cloned.1.call-start
  76.3 29.4 %reduce-scatter.5.cloned.1.call-done = f32[256,256]{1,0:T(8,128)} async-done(((f32[256,512]{1,0:T(8,128)}), f32[256,256]{1,0:T(8,128)}) %reduce-scatter.5.cloned.1.call-update) | async-done | bytes 262160 | tf_op jit(solution)/shard_map/reduce_scatter | solution.py:16
  105.7 0.0 copy-done.1
  105.7 1.6 add_convert_fusion
  107.3 0.0 all-gather.5.cloned.1.call-update
  107.4 0.0 all-gather.7.cloned.1.call-start
  107.4 0.5 all-gather.7.cloned.1.call-update
  107.9 0.0 all-gather.9.cloned.1.call-start
  108.0 0.5 all-gather.9.cloned.1.call-update
  108.5 0.0 all-gather.11.cloned.1.call-start
  108.6 0.5 all-gather.11.cloned.1.call-update
  109.1 0.0 copy-done.2
  109.1 0.0 copy-done.3
  109.2 104.9 %all-gather.5.cloned.1.call-done = bf16[256,4096]{1,0:T(8,128)(2,1)} async-done(((bf16[256,256]{1,0:T(8,128)(2,1)}), bf16[256,4096]{1,0:T(8,128)(2,1)}) %all-gather.5.cloned.1.call-update) | async-done | bytes 2097168 | tf_op jit(solution)/shard_map/all_gather | solution.py:77
  214.1 2.1 fusion.3
  216.2 0.0 copy-start.4
  216.2 64.1 %all-gather.7.cloned.1.call-done = bf16[1,4096,1024]{2,1,0:T(8,128)(2,1)} async-done(((bf16[1,128,1024]{2,1,0:T(8,128)(2,1)}), bf16[1,4096,1024]{2,1,0:T(8,128)(2,1)}) %all-gather.7.cloned.1.call-update) | async-done | bytes 8388624 | tf_op jit(solution)/shard_map/all_gather | solution.py:83
  280.2 7.4 %fusion.1 = f32[256,1024]{1,0:T(8,128)} fusion(bf16[1,4096,1024]{2,1,0:T(8,128)(2,1)} %all-gather.7.cloned.1.call-done, bf16[256,4096]{1,0:T(8,128)(2,1)} %all-gather.5.cloned.1.call-done, f32[4096]{0:T(1024)S(1)} %convert_element_type.60, f32[256]{0:T(256)S(1)} %add_rsqrt_fusion.1), kind=kOutput, calls=%fused_computation.1 | convolution fusion | flops 2151677952 | bytes 11551744 | tf_op jit(solution)/shard_map/dot_general | solution.py:81
  287.6 56.1 %all-gather.9.cloned.1.call-done = bf16[1,1024,1024]{2,1,0:T(8,128)(2,1)} async-done(((bf16[1,32,1024]{2,1,0:T(8,128)(2,1)}), bf16[1,1024,1024]{2,1,0:T(8,128)(2,1)}) %all-gather.9.cloned.1.call-update) | async-done | bytes 2097168 | tf_op jit(solution)/shard_map/all_gather | solution.py:50
  343.8 0.0 copy-done.4
  343.8 3.4 fusion.26
  347.2 61.2 %all-gather.11.cloned.1.call-done = bf16[1,1024,1536]{2,1,0:T(8,128)(2,1)} async-done(((bf16[1,32,1536]{2,1,0:T(8,128)(2,1)}), bf16[1,1024,1536]{2,1,0:T(8,128)(2,1)}) %all-gather.11.cloned.1.call-update) | async-done | bytes 3145744 | tf_op jit(solution)/shard_map/all_gather | solution.py:93
  408.4 4.0 fusion.8
  412.4 10.9 %all-to-all-start = ((bf16[16,16,1,1536]{3,1,2,0:T(8,128)(2,1)}), bf16[16,16,1,1536]{3,1,2,0:T(8,128)(2,1)}, u32[]{:S(2)}, u32[]{:S(2)}) async-start(bf16[16,16,1,1536]{3,1,2,0:T(8,128)(2,1)} %bitcast.38), calls=%async_computation.2 | async-start | bytes 1572864 | tf_op jit(solution)/shard_map/all_to_all | solution.py:97
  423.2 23.6 %all-to-all-done = bf16[16,16,1,1536]{3,1,2,0:T(8,128)(2,1)} async-done(((bf16[16,16,1,1536]{3,1,2,0:T(8,128)(2,1)}), bf16[16,16,1,1536]{3,1,2,0:T(8,128)(2,1)}, u32[]{:S(2)}, u32[]{:S(2)}) %all-to-all-start) | async-done | bytes 786464 | tf_op jit(solution)/shard_map/all_to_all | solution.py:97
  446.9 2.0 fusion.46
  448.8 2.1 reshape.45
  450.9 2.1 reshape.46
  453.0 1.1 reshape.44
  454.1 3.2 fusion.47
  457.3 1.9 fusion.25
  459.2 0.9 copy.26
  460.1 2.1 convert_element_type.69
  (5 shorter events, 0.0 us)
Async XLA Ops:
  6.5 1.9 copy-start
  6.5 69.7 %reduce-scatter.3.cloned.1.call-start = ((), (), s32[]{:S(2)}) async-start(), calls=%async_computation.3 | async-start | bytes 4718592 | tf_op jit(solution)/shard_map/reduce_scatter | solution.py:16
  12.7 93.0 %copy-start.1 = (bf16[256,256]{1,0:T(8,128)(2,1)S(1)}, bf16[256,256]{1,0:T(8,128)(2,1)}, u32[]{:S(2)}) copy-start(bf16[256,256]{1,0:T(8,128)(2,1)} %param.13) | copy-start | bytes 393220
  12.7 96.4 %copy-start.2 = (bf16[4096]{0:T(1024)(128)(2,1)S(1)}, bf16[4096]{0:T(1024)(128)(2,1)}, u32[]{:S(2)}) copy-start(bf16[4096]{0:T(1024)(128)(2,1)} %param.14) | copy-start | bytes 24580
  12.7 96.5 %copy-start.3 = (bf16[1,1024]{1,0:T(2,128)(2,1)S(1)}, bf16[1,1024]{1,0:T(2,128)(2,1)}, u32[]{:S(2)}) copy-start(bf16[1,1024]{1,0:T(2,128)(2,1)} %param.18) | copy-start | bytes 6148
  12.7 93.0 %reduce-scatter.5.cloned.1.call-start = ((), (), s32[]{:S(2)}) async-start(), calls=%async_computation.4 | async-start | bytes 786432 | tf_op jit(solution)/shard_map/reduce_scatter | solution.py:16
  76.2 137.8 %all-gather.5.cloned.1.call-start = ((), (), s32[]{:S(2)}) async-start(), calls=%async_computation.5 | async-start | bytes 2228224 | tf_op jit(solution)/shard_map/all_gather | solution.py:77
  107.4 172.9 %all-gather.7.cloned.1.call-start = ((), (), s32[]{:S(2)}) async-start(), calls=%async_computation.6 | async-start | bytes 8650752 | tf_op jit(solution)/shard_map/all_gather | solution.py:83
  107.9 235.8 %all-gather.9.cloned.1.call-start = ((), (), s32[]{:S(2)}) async-start(), calls=%async_computation.7 | async-start | bytes 2162688 | tf_op jit(solution)/shard_map/all_gather | solution.py:50
  108.5 299.8 %all-gather.11.cloned.1.call-start = ((), (), s32[]{:S(2)}) async-start(), calls=%async_computation.8 | async-start | bytes 3244032 | tf_op jit(solution)/shard_map/all_gather | solution.py:93
  216.2 127.6 %copy-start.4 = (s32[256,1]{0,1:T(1,128)S(1)}, s32[256,1]{0,1:T(1,128)}, u32[]{:S(2)}) copy-start(s32[256,1]{0,1:T(1,128)} %param.17) | copy-start | bytes 3076
  412.4 34.5 %all-to-all-start = ((bf16[16,16,1,1536]{3,1,2,0:T(8,128)(2,1)}), bf16[16,16,1,1536]{3,1,2,0:T(8,128)(2,1)}, u32[]{:S(2)}, u32[]{:S(2)}) async-start(bf16[16,16,1,1536]{3,1,2,0:T(8,128)(2,1)} %bitcast.38), calls=%async_computation.2 | async-start | bytes 1572864 | tf_op jit(solution)/shard_map/all_to_all | solution.py:97
Sparse Core Ops, SparseCore 0:
  12.8 63.3 reduce-scatter.2
  79.0 26.6 reduce-scatter.4
  108.8 105.2 all-gather.4
  216.1 64.1 all-gather.6
  282.2 61.4 all-gather.8
  345.8 62.5 all-gather.10
where the time goes:
time: 475 us; the launch traced here: 469 us
  waiting for transfers between devices  404 us (85%)
  matrix products  24.1 us (5%)
  between operations  13.5 us (3%)
  local copies, waits for them, and re-layouts  12.1 us (3%)
  starting transfers between devices  11 us (2%)
    all_gather x1, waiting for transfers between devices, per_device(): whole = lax.all_gather(temporal, BOOK, axis=1, tiled=True)  105 us
    reduce_scatter x2, waiting for transfers between devices, sum_by_axis(): nearer = lax.psum_scatter(shard, axes[0], scatter_dimension=dim, tiled=True)  92.9 us
    all_gather x1, waiting for transfers between devices, per_device(): lax.all_gather(in_proj, 'frames', axis=1, tiled=True)[0]  64.1 us
    all_gather x1, waiting for transfers between devices, per_device(): lax.all_gather(qkv_weight, 'frames', axis=1, tiled=True)[0]  61.2 us
    all_gather x1, waiting for transfers between devices, gather_embedding(): table_piece = lax.all_gather(embedding, 'frames', axis=1, tiled=True)  56.1 us
    all_to_all x1, waiting for transfers between devices, per_device(): lax.all_to_all(grouped, BOOK, split_axis=0, concat_axis=2, tiled=True)  23.6 us
    all_to_all x1, starting transfers between devices, per_device(): lax.all_to_all(grouped, BOOK, split_axis=0, concat_axis=2, tiled=True)  10.9 us
  transfers between devices with their start and end apart: 7, of which 7 were waited for; matrix products, arithmetic and copies ran while one was open for 3% of the time, Pallas kernels for 0%

commit v1 on v0

v1 whole, which is shorter than its diff:
```python
import functools

import jax
import jax.numpy as jnp
from jax import lax
from jax.experimental import pallas as pl
from jax.experimental.pallas import tpu as pltpu
from jax.sharding import PartitionSpec as P

H = 8
HD = 64
WIDTH = H * HD
MESH = pl.DeviceIdType.MESH
F32 = jnp.float32
BF16 = jnp.bfloat16


def coords():
    f = lax.axis_index("frames")
    b = lax.axis_index("book")
    core = lax.rem(f, 2)
    y_lo = lax.rem(f // 2, 4)
    x = f // 8
    return x, lax.rem(b, 2) * 4 + y_lo, b // 2, core


def dev(x, y, z, core):
    return {"frames": x * 8 + lax.rem(y, 4) * 2 + core, "book": z * 2 + y // 4}


def send(src, dst, ssem, rsem, target):
    return pltpu.make_async_remote_copy(
        src_ref=src, dst_ref=dst, send_sem=ssem, recv_sem=rsem,
        device_id=target, device_id_type=MESH,
    )


def mod8(v):
    return lax.rem(v + 16, 8)


def barrier(targets, count):
    sem = pltpu.get_barrier_semaphore()
    for target in targets:
        pl.semaphore_signal(sem, inc=1, device_id=target, device_id_type=MESH)
    pl.semaphore_wait(sem, count)


def mix_kernel(gate, up, dw, res, out, hid, own, a_s, a_r, zs, ys, y_rel, y_r, tf,
               a_ss, a_rs, y_ss, y_rs, b_ss, b_rs, o_sem):
    x, y, z, core = coords()
    y_hi = y // 4
    zn = (dev(x, y, mod8(z + 1), core), dev(x, y, mod8(z - 1), core))
    yn = (dev(x, mod8(y + 2), z, core), dev(x, mod8(y - 2), z, core))
    barrier(zn + yn, 4)

    g = gate[...].astype(F32)
    hid[...] = (g / (1.0 + jnp.exp(-g)) * up[...].astype(F32)).astype(BF16)
    sent = []

    def a_copy(d, u, s):
        return send(a_s.at[d, u, s], a_r.at[d, u, s], a_ss.at[d, u, s], a_rs.at[d, u, s], zn[d])

    def y_copy(d, u):
        return send(ys.at[d, u], y_rel.at[d, u], y_ss.at[0, d, u], y_rs.at[0, d, u], yn[d])

    def y_copy2(d, u):
        return send(y_rel.at[d, u], y_r.at[d, u], y_ss.at[1, d, u], y_rs.at[1, d, u], yn[d])

    for s in range(8):
        for d in (0, 1):
            blk = mod8(z - 1 - s) if d == 0 else mod8(z + 1 + s)
            cols = pl.ds(pl.multiple_of(blk * 512, 512), 512)
            own[d] = jnp.dot(hid[d * 128:(d + 1) * 128, :], dw[:, cols],
                             preferred_element_type=F32).reshape(2, 64, 512)
        for u in (0, 1):
            for d in (0, 1):
                val = own[d, u]
                if s > 0:
                    a_copy(d, u, s - 1).wait_recv()
                    val = val + a_r[d, u, s - 1].astype(F32)
                if s < 7:
                    a_s[d, u, s] = val.astype(BF16)
                    copy = a_copy(d, u, s)
                    copy.start()
                    sent.append(copy)
                else:
                    zs[d, u] = val
                    cols = pl.ds(pl.multiple_of(y_hi * 256, 256), 256)
                    rows = pl.ds(d * 128 + u * 64, 64)
                    zs[d, u, :, cols] = zs[d, u, :, cols] + res[rows, :].astype(F32)
                    ys[d, u] = zs[d, u].astype(BF16)
                    copy = y_copy(d, u)
                    copy.start()
                    sent.append(copy)
    for u in (0, 1):
        for d in (0, 1):
            y_copy(d, u).wait_recv()
            copy = y_copy2(d, u)
            copy.start()
            sent.append(copy)

    def b_copy(d, s, h):
        blk = mod8(z - s) if d == 0 else mod8(z + s)
        ref = tf.at[blk, h]
        return send(ref, ref, b_ss.at[d, s, h], b_rs.at[d, s, h], zn[d])

    for d in (0, 1):
        for u in (0, 1):
            y_copy2(d, u).wait_recv()
            tf[z, d, u * 64:(u + 1) * 64, :] = (zs[d, u] + y_r[d, u].astype(F32)).astype(BF16)
        for way in (0, 1):
            copy = b_copy(way, 0, d)
            copy.start()
            sent.append(copy)
    for s in range(1, 5):
        for h in (0, 1):
            for d in (0, 1):
                if s == 4 and h != d:
                    continue
                b_copy(d, s - 1, h).wait_recv()
                if s < 3 or (s == 3 and h == d):
                    copy = b_copy(d, s, h)
                    copy.start()
                    sent.append(copy)
    for copy in sent:
        copy.wait_send()
    done = pltpu.make_async_copy(tf, out, o_sem)
    done.start()
    done.wait()


def mix(gate, up, dw, res):
    vmem = pl.BlockSpec(memory_space=pltpu.VMEM)
    dma = pltpu.SemaphoreType.DMA
    return pl.pallas_call(
        mix_kernel,
        name="mix",
        out_shape=jax.ShapeDtypeStruct((8, 2, 128, 512), BF16),
        in_specs=[vmem] * 4,
        out_specs=pl.BlockSpec(memory_space=pl.ANY),
        scratch_shapes=[
            pltpu.VMEM((256, 384), BF16),
            pltpu.VMEM((2, 2, 64, 512), F32),
            pltpu.VMEM((2, 2, 7, 64, 512), BF16),
            pltpu.VMEM((2, 2, 7, 64, 512), BF16),
            pltpu.VMEM((2, 2, 64, 512), F32),
            pltpu.VMEM((2, 2, 64, 512), BF16),
            pltpu.VMEM((2, 2, 64, 512), BF16),
            pltpu.VMEM((2, 2, 64, 512), BF16),
            pltpu.VMEM((8, 2, 128, 512), BF16),
            dma((2, 2, 7)), dma((2, 2, 7)),
            dma((2, 2, 2)), dma((2, 2, 2)),
            dma((2, 4, 2)), dma((2, 4, 2)),
            dma,
        ],
        compiler_params=pltpu.CompilerParams(collective_id=0, has_side_effects=True),
        cost_estimate=pl.CostEstimate(flops=10**9, bytes_accessed=100 * 2**20, transcendentals=0),
    )(gate, up, dw, res)


def depth_kernel(tf, gain, w, emb, tok, dgain, qw, out, xb, acc, packed, q_all, qp, rel,
                 d_ss, d_rs, r_ss, r_rs):
    x, y, z, core = coords()
    y_hi = y // 4
    b = z * 2 + y_hi
    up, down = mod8(y + 2), mod8(y - 2)
    peers = [dev(x, y, mod8(z - i), core) for i in range(1, 8)]
    peers += [dev(x, down, mod8(z - i), core) for i in range(4)]
    peers += [dev(x, up, z, core)]
    peers += [dev(x, up, mod8(z - i), core) for i in range(4, 8)]
    barrier(peers, len(peers))

    acc[...] = jnp.zeros_like(acc)

    def block(i, total):
        v = tf[i].reshape(256, 512).astype(F32)
        xb[...] = (v * gain[i].astype(F32)).astype(BF16)

        def tile(n, carry):
            cols = pl.ds(pl.multiple_of(n * 256, 256), 256)
            rows = pl.ds(pl.multiple_of(i * 512, 512), 512)
            acc[:, cols] += jnp.dot(xb[...], w[rows, cols], preferred_element_type=F32)
            return carry

        lax.fori_loop(0, 4, tile, 0)
        return total + jnp.sum(v * v, axis=-1, keepdims=True)

    total = lax.fori_loop(0, 8, block, jnp.zeros((256, 1), F32))
    scale = lax.rsqrt(total * (1.0 / 4096) + 1e-05)
    columns = lax.broadcasted_iota(jnp.int32, (256, 1024), 1)
    matches = jnp.where(tok[...] == columns, 1.0, 0.0).astype(BF16)
    depth = (acc[...] * scale + jnp.dot(matches, emb[...], preferred_element_type=F32)).astype(BF16)
    depth = depth.astype(F32)
    moment = jnp.mean(depth * depth, axis=-1, keepdims=True)
    normed = (depth * lax.rsqrt(moment + 1e-05) * dgain[...].astype(F32)).astype(BF16)
    packed[...] = jnp.dot(normed, qw[...], preferred_element_type=F32).astype(BF16)

    def rows_of(zz, plane):
        return pl.ds(pl.multiple_of((zz * 2 + plane) * 16, 16), 16)

    def slot(zz, plane):
        return q_all.at[rows_of(zz, plane)]

    sent = []

    def go(copy):
        copy.start()
        sent.append(copy)

    def first(i):
        way = i // 4
        return send(packed.at[rows_of(mod8(z + i), 1 - y_hi)], rel.at[i],
                    r_ss.at[i], r_rs.at[i], dev(x, (up, down)[way], z, core))

    def second(i):
        way = i // 4
        source = (down, up)[way] // 4
        return send(rel.at[i], slot(z, source), d_ss.at[8 + i], d_rs.at[8 + i],
                    dev(x, (up, down)[way], mod8(z + i), core))

    def direct(i):
        return send(packed.at[rows_of(mod8(z + i), y_hi)], slot(z, y_hi),
                    d_ss.at[i], d_rs.at[i], dev(x, y, mod8(z + i), core))

    for i in (3, 4, 2, 5, 1, 6, 0, 7):
        go(first(i))
    for i in (4, 3, 5, 2, 6, 1, 7):
        go(direct(i))
    q_all[rows_of(z, y_hi), :] = packed[rows_of(z, y_hi), :]
    for i in (3, 4, 2, 5, 1, 6, 0, 7):
        first(i).wait_recv()
        go(second(i))
    for i in range(1, 8):
        direct(i).wait_recv()
    for i in range(8):
        second(i).wait_recv()

    row = lax.broadcasted_iota(jnp.int32, (256, 256), 0)
    col = lax.broadcasted_iota(jnp.int32, (256, 256), 1)
    same = lax.rem(col, 16) == row // 16
    swap = jnp.where(same & (col // 16 == lax.rem(row, 16)), HD ** -0.5, 0.0).astype(BF16)
    seen = same & (col // 16 <= lax.rem(row, 16))
    qp[...] = jnp.dot(swap, q_all[:, :WIDTH], preferred_element_type=F32).astype(BF16)
    for h in range(0, H, 2):
        pair = []
        for k in (h, h + 1):
            keys = q_all[:, WIDTH + k * HD:WIDTH + (k + 1) * HD]
            values = q_all[:, 2 * WIDTH + k * HD:2 * WIDTH + (k + 1) * HD]
            scores = lax.dot_general(qp[:, k * HD:(k + 1) * HD], keys, (((1,), (1,)), ((), ())),
                                     preferred_element_type=F32)
            scores = jnp.where(seen, scores, -1e30)
            expo = jnp.exp(scores - jnp.max(scores, axis=-1, keepdims=True))
            share = expo / jnp.sum(expo, axis=-1, keepdims=True)
            pair.append(jnp.dot(share.astype(BF16), values, preferred_element_type=F32))
        out[:, h * HD:(h + 2) * HD] = jnp.concatenate(pair, axis=1).astype(BF16)
    for copy in sent:
        copy.wait_send()


def depth_stage(tf, gain, w, emb, tok, dgain, qw):
    vmem = pl.BlockSpec(memory_space=pltpu.VMEM)
    dma = pltpu.SemaphoreType.DMA
    return pl.pallas_call(
        depth_kernel,
        name="depth",
        out_shape=jax.ShapeDtypeStruct((256, WIDTH), BF16),
        in_specs=[vmem] * 7,
        out_specs=vmem,
        scratch_shapes=[
            pltpu.VMEM((256, 512), BF16),
            pltpu.VMEM((256, 1024), F32),
            pltpu.VMEM((256, 3 * WIDTH), BF16),
            pltpu.VMEM((256, 3 * WIDTH), BF16),
            pltpu.VMEM((256, WIDTH), BF16),
            pltpu.VMEM((8, 16, 3 * WIDTH), BF16),
            dma((16,)), dma((16,)), dma((8,)), dma((8,)),
        ],
        compiler_params=pltpu.CompilerParams(collective_id=1, has_side_effects=True),
        cost_estimate=pl.CostEstimate(flops=4 * 10**9, bytes_accessed=20 * 2**20, transcendentals=0),
    )(tf, gain, w, emb, tok, dgain, qw)


def per_device(gate_pre, up_pre, down_weight, residual, out_gain, in_proj, embedding, token_ids,
               depth_gain, qkv_weight):
    own = jnp.concatenate(
        [in_proj[0], embedding[0], qkv_weight[0].reshape(48, 1024)], axis=0)
    every = lax.all_gather(own, "frames", axis=0)
    tf = mix(gate_pre, up_pre, down_weight, residual)
    w = every[:, :128].reshape(4096, 1024)
    emb = every[:, 128:160].reshape(1024, 1024)
    qw = every[:, 160:].reshape(1024, 1536)
    out = depth_stage(tf, out_gain.reshape(8, 1, 512), w, emb, token_ids, depth_gain, qw)
    return out.reshape(16, 16, WIDTH)


def solution(mesh):
    placed = (
        P("frames", "book"),
        P("frames", "book"),
        P("book", None),
        P("frames", "book"),
        P(),
        P("book", "frames", None),
        P("book", "frames", None),
        P("frames", "book"),
        P("book", None),
        P("book", "frames", None),
    )
    return jax.shard_map(per_device, mesh=mesh, in_specs=placed,
                         out_specs=P(("frames", "book"), None, None), check_vma=False)
```

time: 475 us -> 192 us (0.40)
  waiting for transfers between devices: 404 us -> 17.2 us
  Pallas kernels: 0 us -> 135 us
  matrix products: 24.1 us -> 0 us
  starting transfers between devices: 11 us -> 0.01 us
  local copies, waits for them, and re-layouts: 12.1 us -> 22.4 us
    all_gather x4 -> x1, waiting for transfers between devices: 286 us -> 17.2 us  [per_device(): every = lax.all_gather(own, 'frames', axis=0)]
    pallas_call x0 -> x2, Pallas kernels: none -> 135 us  [the longest x1 82.5 us: mix(): pl.pallas_call(mix_kernel, name='mix', out_shape=jax.ShapeDtypeStruct((8,...]
    reduce_scatter x2 -> x0, waiting for transfers between devices: 92.9 us -> none  [sum_by_axis(): nearer = lax.psum_scatter(shard, axes[0], scatter_dimension=dim, tiled=True)]
    all_to_all x1 -> x0, waiting for transfers between devices: 23.6 us -> none  [per_device(): lax.all_to_all(grouped, BOOK, split_axis=0, concat_axis=2, tiled=True)]
    dot_general x5 -> x0, matrix products: 20.9 us -> none  [the longest x1 7.37 us: per_device(): jnp.dot(columns, lax.all_gather(in_proj, 'frames', axis=1, tiled=True)[0]...]
    slice x1 -> x3, local copies, waits for them, and re-layouts: 1.96 us -> 13.8 us  [the longest x1 8.21 us: per_device(): w = every[:, :128].reshape(4096, 1024)]
    all_to_all x1 -> x0, starting transfers between devices: 10.9 us -> none  [per_device(): lax.all_to_all(grouped, BOOK, split_axis=0, concat_axis=2, tiled=True)]
  transfers between devices with their start and end apart: 7 -> 1, of which waited for: 7 -> 1; matrix products, arithmetic and copies ran while one was open for 3% -> 1% of each run, Pallas kernels for 0% -> 44%
where the time goes in v1:
time: 192 us; the launch traced here: 190 us
  Pallas kernels  135 us (70%)
  local copies, waits for them, and re-layouts  22.4 us (12%)
  waiting for transfers between devices  17.2 us (9%)
  between operations  13.4 us (7%)
    pallas_call x1, Pallas kernels, mix(): pl.pallas_call(mix_kernel, name='mix', out_shape=jax.ShapeDtypeStruct((8,...  82.5 us
    pallas_call x1, Pallas kernels, depth_stage(): pl.pallas_call(depth_kernel, name='depth', out_shape=jax.ShapeDtypeStruct...  52.3 us
    all_gather x1, waiting for transfers between devices, per_device(): every = lax.all_gather(own, 'frames', axis=0)  17.2 us
    slice x1, local copies, waits for them, and re-layouts, per_device(): w = every[:, :128].reshape(4096, 1024)  8.21 us
  transfers between devices with their start and end apart: 1, of which 1 were waited for; matrix products, arithmetic and copies ran while one was open for 1% of the time, Pallas kernels for 44%

profile of v1, /device:TPU:6, one launch (start us, length us, event | category | flops | bytes accessed | tf_op | source)
XLA Modules:
  0.0 189.6 jit_solution(2263896774086996880)
XLA Ops:
  6.5 0.0 all-gather.3.cloned.1.call-start
  6.5 1.0 reshape_squeeze.3
  7.5 1.8 pad_maximum_fusion
  9.3 0.0 all-gather.3.cloned.1.call-update
  9.3 1.5 copy.13.tok
  10.8 1.3 reshape.21.gain
  12.1 82.5 %mix.1.tf = bf16[8,2,128,512]{3,2,1,0:T(8,128)(2,1)} custom-call(bf16[256,384]{1,0:T(8,128)(2,1)} %gate.1, bf16[256,384]{1,0:T(8,128)(2,1)} %up.1, bf16[384,4096]{1,0:T(8,128)(2,1)} %dw.1, bf16[256,256]{1,0:T(8,128)(2,1)} %res.1), custom_call_target="tpu_custom_call" | custom-call | flops 1000000000 | bytes 104857600 | tf_op jit(solution)/shard_map/mix/pallas_call | solution.py:136
  94.6 17.2 %all-gather.3.cloned.1.call-done = bf16[6656,1024]{1,0:T(8,128)(2,1)} async-done(((bf16[208,1024]{1,0:T(8,128)(2,1)}), bf16[6656,1024]{1,0:T(8,128)(2,1)}) %all-gather.3.cloned.1.call-update) | async-done | bytes 13631504 | tf_op jit(solution)/shard_map/all_gather | solution.py:288
  111.9 8.2 %slice.12 = bf16[32,128,1024]{2,1,0:T(8,128)(2,1)} slice(bf16[32,208,1024]{2,1,0:T(8,128)(2,1)} %bitcast.7), slice={[0:32], [0:128], [0:1024]} | slice | bytes 16777216 | tf_op jit(solution)/shard_map/slice | solution.py:290
  120.1 2.3 %slice.14 = bf16[32,48,1024]{2,1,0:T(8,128)(2,1)S(1)} slice(bf16[32,208,1024]{2,1,0:T(8,128)(2,1)} %bitcast.8), slice={[0:32], [160:208], [0:1024]} | slice | bytes 6291456 | tf_op jit(solution)/shard_map/slice | solution.py:292
  122.4 3.3 %slice.13 = bf16[32,32,1024]{2,1,0:T(8,128)(2,1)} slice(bf16[32,208,1024]{2,1,0:T(8,128)(2,1)} %bitcast.9), slice={[0:32], [128:160], [0:1024]} | slice | bytes 4194304 | tf_op jit(solution)/shard_map/slice | solution.py:291
  125.6 3.2 %reshape.18.qw = bf16[1024,1536]{1,0:T(8,128)(2,1)} reshape(bf16[32,48,1024]{2,1,0:T(8,128)(2,1)S(1)} %slice.14) | data formatting | bytes 6291456 | tf_op jit(solution)/shard_map/reshape | solution.py:292
  128.8 52.3 %depth.1 = bf16[256,512]{1,0:T(8,128)(2,1)} custom-call(bf16[8,2,128,512]{3,2,1,0:T(8,128)(2,1)} %mix.1.tf, bf16[8,1,512]{2,1,0:T(2,128)(2,1)} %reshape.21.gain, bf16[4096,1024]{1,0:T(8,128)(2,1)} %bitcast.6, bf16[1024,1024]{1,0:T(8,128)(2,1)} %bitcast.10, s32[256,1]{1,0:T(8,128)} %copy.13.tok, bf16[1,1024]{1,0:T(2,128)(2,1)} %dgain.1, ...), custom_call_target="tpu_custom_call" | custom-call | flops 4000000000 | bytes 20971520 | tf_op jit(solution)/shard_map/depth/pallas_call | solution.py:264
  181.1 1.7 copy.15
Async XLA Ops:
  6.5 105.3 %all-gather.3.cloned.1.call-start = ((), (), s32[]{:S(2)}) async-start(), calls=%async_computation | async-start | bytes 14057472 | tf_op jit(solution)/shard_map/all_gather | solution.py:288
Sparse Core Ops, SparseCore 0:
  9.5 102.3 all-gather.2

commit v2 on v1

v2 whole, which is shorter than its diff:
```python
import jax
import jax.numpy as jnp
from jax import lax
from jax.experimental import pallas as pl
from jax.experimental.pallas import tpu as pltpu
from jax.sharding import PartitionSpec as P

H = 8
HD = 64
WIDTH = H * HD
MESH = pl.DeviceIdType.MESH
F32 = jnp.float32
BF16 = jnp.bfloat16
SHARD_ROWS = (128, 32, 32)


def dev(x, y, z, core):
    return {"frames": x * 8 + lax.rem(y, 4) * 2 + core, "book": z * 2 + y // 4}


def send(src, dst, ssem, rsem, target):
    return pltpu.make_async_remote_copy(
        src_ref=src, dst_ref=dst, send_sem=ssem, recv_sem=rsem,
        device_id=target, device_id_type=MESH,
    )


def mod8(v):
    return lax.rem(v + 16, 8)


def mod4(v):
    return lax.rem(v + 8, 4)


def kernel(gate_in, up_in, dw_in, res_in, gain, w_in, e_in, q_in, tok, dgain, out,
           gate, up, dw, res, hid, own, a_s, a_r, zs, ys, y_rel, y_r, tf, wbuf, ebuf, qbuf,
           xb, acc, looked, packed, q_all, qp, rel,
           in_sem, own_sem, a_ss, a_rs, y_ss, y_rs, b_ss, b_rs, c_ss, c_rs, p_rs,
           d_ss, d_rs, r_ss, r_rs):
    f = lax.axis_index("frames")
    b = lax.axis_index("book")
    core = lax.rem(f, 2)
    yl = lax.rem(f // 2, 4)
    x = f // 8
    y_hi = lax.rem(b, 2)
    z = b // 2
    y = y_hi * 4 + yl
    mid = (yl + 1) // 2 == 1
    order = (yl, yl + 1 - 2 * lax.rem(yl, 2), 2 - yl // 2, 3 * (1 - yl // 2))
    zn = (dev(x, y, mod8(z + 1), core), dev(x, y, mod8(z - 1), core))
    yn = (dev(x, mod8(y + 2), z, core), dev(x, mod8(y - 2), z, core))
    xn = (dev(mod4(x + 1), y, z, core), dev(mod4(x - 1), y, z, core))
    near = dev(x, y_hi * 4 + order[1], z, core)
    inner = dev(x, y_hi * 4 + 3 - yl, z, core)
    twin = dev(x, y, z, 1 - core)
    way_up, way_down = mod8(y + 2), mod8(y - 2)

    weights = (wbuf, ebuf, qbuf)
    shards = (w_in, e_in, q_in)

    def c_slot(a, bx, by, half=None, c=core):
        rows = SHARD_ROWS[a]
        start = ((bx * 4 + by) * 2 + c) * rows
        if half is not None:
            rows //= 2
            start = start + half * rows
        return weights[a].at[pl.ds(pl.multiple_of(start, rows), rows)]

    loads = [pltpu.make_async_copy(src, dst, in_sem.at[i]) for i, (src, dst) in enumerate(
        ((gate_in, gate), (up_in, up), (dw_in, dw), (res_in, res)))]
    places = [pltpu.make_async_copy(shards[a].at[0], c_slot(a, x, yl), own_sem.at[a])
              for a in range(3)]
    for copy in loads + places:
        copy.start()

    peers = [dev(x, y, mod8(z - i), core) for i in range(1, 8)]
    peers += [dev(x, way_down, mod8(z - i), core) for i in range(4)]
    peers += [dev(x, way_up, z, core)]
    peers += [dev(x, way_up, mod8(z - i), core) for i in range(4, 8)]
    peers += [xn[0], xn[1], near, twin]
    sem = pltpu.get_barrier_semaphore()
    for peer in peers:
        pl.semaphore_signal(sem, inc=1, device_id=peer, device_id_type=MESH)

    @pl.when(mid)
    def _():
        pl.semaphore_signal(sem, inc=1, device_id=inner, device_id_type=MESH)

    pl.semaphore_wait(sem, len(peers) + lax.rem((yl + 1) // 2, 2))

    sent = []
    sent_mid = []

    def go(copy):
        copy.start()
        sent.append(copy)

    def c_copy(a, n, src, bx, by, target, half=None):
        return send(src, c_slot(a, bx, by, half), c_ss.at[a, n],
                    c_rs.at[a, bx, by, 0 if half is None else half], target)

    def c_twin(a, n, src, bx, by):
        return send(src, c_slot(a, bx, by), c_ss.at[a, n], p_rs.at[a, bx, by], twin)

    def c_go_mid(copy):
        @pl.when(mid)
        def _():
            copy.start()
        sent_mid.append(copy)

    def c_own(a):
        src = shards[a].at[0]
        for d in (0, 1):
            go(c_copy(a, d, src, x, yl, xn[d]))
        go(c_copy(a, 2, src, x, yl, near))
        c_go_mid(c_copy(a, 3, src, x, yl, inner))
        go(c_twin(a, 4, src, x, yl))

    def c_wait(a, bx, by, half=None):
        c_copy(a, 0, c_slot(a, bx, by, half), bx, by, twin, half).wait_recv()

    def c_col(a, i):
        by = order[i]
        src = c_slot(a, x, by)
        c_wait(a, x, by)
        n = 5 + (i - 1) * 4
        for d in (0, 1):
            go(c_copy(a, n + d, src, x, by, xn[d]))
        target = dev(x, y_hi * 4 + (3 - yl), z, core) if i == 1 else dev(
            x, y_hi * 4 + mod4((yl - 1) * 3), z, core)
        c_go_mid(c_copy(a, n + 2, src, x, by, target))
        go(c_twin(a, n + 3, src, x, by))

    def c_row(a, i):
        by = order[i]
        n = 17 + i * 4
        for d in (0, 1):
            bx = mod4(x - 1) if d == 0 else mod4(x + 1)
            c_wait(a, bx, by)
            go(c_copy(a, n + d, c_slot(a, bx, by, d), bx, by, xn[d], d))
            go(c_twin(a, n + 2 + d, c_slot(a, bx, by), bx, by))

    def c_far(a, i):
        by = order[i]
        bx = mod4(x + 2)
        for half in (0, 1):
            c_wait(a, bx, by, half)
        go(c_twin(a, 33 + i, c_slot(a, bx, by), bx, by))

    def c_done(a):
        places[a].wait()
        for bx in range(4):
            for by in range(4):
                slot = c_slot(a, bx, by, None, 1 - core)
                send(slot, slot, c_ss.at[a, 0], p_rs.at[a, bx, by], twin).wait_recv()

    def a_copy(d, u, s):
        return send(a_s.at[d, u, s], a_r.at[d, u, s], a_ss.at[d, u, s], a_rs.at[d, u, s], zn[d])

    def y_copy(d, u):
        return send(ys.at[d, u], y_rel.at[d, u], y_ss.at[0, d, u], y_rs.at[0, d, u], yn[d])

    def y_copy2(d, u):
        return send(y_rel.at[d, u], y_r.at[d, u], y_ss.at[1, d, u], y_rs.at[1, d, u], yn[d])

    c_own(0)
    for copy in loads:
        copy.wait()
    g = gate[...].astype(F32)
    hid[...] = (g / (1.0 + jnp.exp(-g)) * up[...].astype(F32)).astype(BF16)

    def after_a(s):
        if s == 1:
            c_col(0, 1)
            c_row(0, 0)
        if s == 3:
            c_col(0, 2)
            c_row(0, 1)
            c_far(0, 0)
        if s == 5:
            c_col(0, 3)
            c_row(0, 2)
            c_far(0, 1)
            c_own(1)
            c_own(2)
        if s == 7:
            c_row(0, 3)
            c_far(0, 2)

    for s in range(8):
        for d in (0, 1):
            blk = mod8(z - 1 - s) if d == 0 else mod8(z + 1 + s)
            cols = pl.ds(pl.multiple_of(blk * 512, 512), 512)
            own[d] = jnp.dot(hid[d * 128:(d + 1) * 128, :], dw[:, cols],
                             preferred_element_type=F32).reshape(2, 64, 512)
        for u in (0, 1):
            for d in (0, 1):
                val = own[d, u]
                if s > 0:
                    a_copy(d, u, s - 1).wait_recv()
                    val = val + a_r[d, u, s - 1].astype(F32)
                if s < 7:
                    a_s[d, u, s] = val.astype(BF16)
                    go(a_copy(d, u, s))
                else:
                    zs[d, u] = val
                    cols = pl.ds(pl.multiple_of(y_hi * 256, 256), 256)
                    rows = pl.ds(d * 128 + u * 64, 64)
                    zs[d, u, :, cols] = zs[d, u, :, cols] + res[rows, :].astype(F32)
                    ys[d, u] = zs[d, u].astype(BF16)
                    go(y_copy(d, u))
        after_a(s)

    for u in (0, 1):
        for d in (0, 1):
            y_copy(d, u).wait_recv()
            go(y_copy2(d, u))
        if u == 0:
            c_far(0, 3)
            for a in (1, 2):
                c_col(a, 1)
                c_row(a, 0)

    def b_copy(d, s, h):
        blk = mod8(z - s) if d == 0 else mod8(z + s)
        ref = tf.at[blk, h]
        return send(ref, ref, b_ss.at[d, s, h], b_rs.at[d, s, h], zn[d])

    def block(i):
        v = tf[i].reshape(256, 512).astype(F32)
        cols = pl.ds(pl.multiple_of(i * 512, 512), 512)
        xb[...] = (v * gain[:, cols].astype(F32)).astype(BF16)

        def tile(n, carry):
            cols = pl.ds(pl.multiple_of(n * 256, 256), 256)
            rows = pl.ds(pl.multiple_of(i * 512, 512), 512)
            acc[:, cols] += jnp.dot(xb[...], wbuf[rows, cols], preferred_element_type=F32)
            return carry

        lax.fori_loop(0, 4, tile, 0)
        return jnp.sum(v * v, axis=-1, keepdims=True)

    for d in (0, 1):
        for u in (0, 1):
            y_copy2(d, u).wait_recv()
            tf[z, d, u * 64:(u + 1) * 64, :] = (zs[d, u] + y_r[d, u].astype(F32)).astype(BF16)
        for way in (0, 1):
            go(b_copy(way, 0, d))
    acc[...] = jnp.zeros_like(acc)
    for a in (1, 2):
        c_col(a, 2)
        c_row(a, 1)
        c_far(a, 0)
    total = jnp.zeros((256, 1), F32)
    for s in range(1, 5):
        for h in (0, 1):
            for d in (0, 1):
                if s == 4 and h != d:
                    continue
                b_copy(d, s - 1, h).wait_recv()
                if s < 3 or (s == 3 and h == d):
                    go(b_copy(d, s, h))
        if s == 1:
            for a in (1, 2):
                c_col(a, 3)
                c_row(a, 2)
                c_far(a, 1)
            c_done(0)
            total = total + block(z)
        if s == 2:
            for a in (1, 2):
                c_row(a, 3)
                c_far(a, 2)
        total = total + block(mod8(z - s))
        if s < 4:
            total = total + block(mod8(z + s))
        if s == 3:
            for a in (1, 2):
                c_far(a, 3)
            c_done(1)
            rows = lax.broadcasted_iota(jnp.int32, (1024, 256), 0)
            matches = jnp.where(tok[...] == rows, 1.0, 0.0).astype(BF16)
            looked[...] = lax.dot_general(matches, ebuf[...], (((0,), (0,)), ((), ())),
                                          preferred_element_type=F32)
            c_done(2)

    scale = lax.rsqrt(total * (1.0 / 4096) + 1e-05)
    depth = (acc[...] * scale + looked[...]).astype(BF16).astype(F32)
    moment = jnp.mean(depth * depth, axis=-1, keepdims=True)
    normed = (depth * lax.rsqrt(moment + 1e-05) * dgain[...].astype(F32)).astype(BF16)
    packed[...] = jnp.dot(normed, qbuf[...], preferred_element_type=F32).astype(BF16)

    def rows_of(zz, plane):
        return pl.ds(pl.multiple_of((zz * 2 + plane) * 16, 16), 16)

    def slot(zz, plane):
        return q_all.at[rows_of(zz, plane)]

    def first(i):
        return send(packed.at[rows_of(mod8(z + i), 1 - y_hi)], rel.at[i],
                    r_ss.at[i], r_rs.at[i], yn[i // 4])

    def second(i):
        source = (way_down, way_up)[i // 4] // 4
        return send(rel.at[i], slot(z, source), d_ss.at[8 + i], d_rs.at[8 + i],
                    dev(x, (way_up, way_down)[i // 4], mod8(z + i), core))

    def direct(i):
        return send(packed.at[rows_of(mod8(z + i), y_hi)], slot(z, y_hi),
                    d_ss.at[i], d_rs.at[i], dev(x, y, mod8(z + i), core))

    for i in (3, 4, 2, 5, 1, 6, 0, 7):
        go(first(i))
    for i in (4, 3, 5, 2, 6, 1, 7):
        go(direct(i))
    q_all[rows_of(z, y_hi), :] = packed[rows_of(z, y_hi), :]
    for i in (3, 4, 2, 5, 1, 6, 0, 7):
        first(i).wait_recv()
        go(second(i))
    for i in range(1, 8):
        direct(i).wait_recv()
    for i in range(8):
        second(i).wait_recv()

    row = lax.broadcasted_iota(jnp.int32, (256, 256), 0)
    col = lax.broadcasted_iota(jnp.int32, (256, 256), 1)
    same = lax.rem(col, 16) == row // 16
    swap = jnp.where(same & (col // 16 == lax.rem(row, 16)), HD ** -0.5, 0.0).astype(BF16)
    seen = same & (col // 16 <= lax.rem(row, 16))
    qp[...] = jnp.dot(swap, q_all[:, :WIDTH], preferred_element_type=F32).astype(BF16)
    for h in range(0, H, 2):
        pair = []
        for k in (h, h + 1):
            keys = q_all[:, WIDTH + k * HD:WIDTH + (k + 1) * HD]
            values = q_all[:, 2 * WIDTH + k * HD:2 * WIDTH + (k + 1) * HD]
            scores = lax.dot_general(qp[:, k * HD:(k + 1) * HD], keys, (((1,), (1,)), ((), ())),
                                     preferred_element_type=F32)
            scores = jnp.where(seen, scores, -1e30)
            expo = jnp.exp(scores - jnp.max(scores, axis=-1, keepdims=True))
            share = expo / jnp.sum(expo, axis=-1, keepdims=True)
            pair.append(jnp.dot(share.astype(BF16), values, preferred_element_type=F32))
        out[:, h * HD:(h + 2) * HD] = jnp.concatenate(pair, axis=1).astype(BF16)
    for copy in sent:
        copy.wait_send()

    @pl.when(mid)
    def _():
        for copy in sent_mid:
            copy.wait_send()


def per_device(gate_pre, up_pre, down_weight, residual, out_gain, in_proj, embedding, token_ids,
               depth_gain, qkv_weight):
    vmem = pl.BlockSpec(memory_space=pltpu.VMEM)
    whole = pl.BlockSpec(memory_space=pl.ANY)
    dma = pltpu.SemaphoreType.DMA
    out = pl.pallas_call(
        kernel,
        name="depth_step",
        out_shape=jax.ShapeDtypeStruct((256, WIDTH), BF16),
        in_specs=[whole] * 4 + [vmem] + [whole] * 3 + [vmem] * 2,
        out_specs=vmem,
        scratch_shapes=[
            pltpu.VMEM((256, 384), BF16),
            pltpu.VMEM((256, 384), BF16),
            pltpu.VMEM((384, 4096), BF16),
            pltpu.VMEM((256, 256), BF16),
            pltpu.VMEM((256, 384), BF16),
            pltpu.VMEM((2, 2, 64, 512), F32),
            pltpu.VMEM((2, 2, 7, 64, 512), BF16),
            pltpu.VMEM((2, 2, 7, 64, 512), BF16),
            pltpu.VMEM((2, 2, 64, 512), F32),
            pltpu.VMEM((2, 2, 64, 512), BF16),
            pltpu.VMEM((2, 2, 64, 512), BF16),
            pltpu.VMEM((2, 2, 64, 512), BF16),
            pltpu.VMEM((8, 2, 128, 512), BF16),
            pltpu.VMEM((4096, 1024), BF16),
            pltpu.VMEM((1024, 1024), BF16),
            pltpu.VMEM((1024, 3 * WIDTH), BF16),
            pltpu.VMEM((256, 512), BF16),
            pltpu.VMEM((256, 1024), F32),
            pltpu.VMEM((256, 1024), F32),
            pltpu.VMEM((256, 3 * WIDTH), BF16),
            pltpu.VMEM((256, 3 * WIDTH), BF16),
            pltpu.VMEM((256, WIDTH), BF16),
            pltpu.VMEM((8, 16, 3 * WIDTH), BF16),
            dma((4,)), dma((3,)),
            dma((2, 2, 7)), dma((2, 2, 7)),
            dma((2, 2, 2)), dma((2, 2, 2)),
            dma((2, 4, 2)), dma((2, 4, 2)),
            dma((3, 40)), dma((3, 4, 4, 2)), dma((3, 4, 4)),
            dma((16,)), dma((16,)), dma((8,)), dma((8,)),
        ],
        compiler_params=pltpu.CompilerParams(collective_id=0, has_side_effects=True),
    )(gate_pre, up_pre, down_weight, residual, out_gain.reshape(1, 4096), in_proj, embedding,
      qkv_weight, token_ids.reshape(1, 256), depth_gain)
    return out.reshape(16, 16, WIDTH)


def solution(mesh):
    placed = (
        P("frames", "book"),
        P("frames", "book"),
        P("book", None),
        P("frames", "book"),
        P(),
        P("book", "frames", None),
        P("book", "frames", None),
        P("frames", "book"),
        P("book", None),
        P("book", "frames", None),
    )
    return jax.shard_map(per_device, mesh=mesh, in_specs=placed,
                         out_specs=P(("frames", "book"), None, None), check_vma=False)
```

time: 192 us -> 131 us (0.68)
  the two profiles are of different devices: /device:TPU:6 before, /device:TPU:87 now
where the time goes in v2:
time: 131 us
  Pallas kernels  128 us (98%)
  local copies, waits for them, and re-layouts  2.98 us (2%)
    pallas_call x1, Pallas kernels, per_device(): pl.pallas_call(kernel, name='depth_step', out_shape=jax.ShapeDtypeStruct(...  128 us

profile of v2, /device:TPU:87, one launch (start us, length us, event | category | flops | bytes accessed | tf_op | source)
XLA Modules:
  0.0 131.3 jit_solution(17649600118064056477)
XLA Ops:
  0.0 1.3 reshape.9.gain
  1.3 128.3 %depth_step.1 = bf16[256,512]{1,0:T(8,128)(2,1)} custom-call(bf16[256,384]{1,0:T(8,128)(2,1)} %gate_in.1, bf16[256,384]{1,0:T(8,128)(2,1)} %up_in.1, bf16[384,4096]{1,0:T(8,128)(2,1)} %dw_in.1, bf16[256,256]{1,0:T(8,128)(2,1)} %res_in.1, bf16[1,4096]{1,0:T(2,128)(2,1)} %reshape.9.gain, bf16[1,128,1024]{2,1,0:T(8,128)(2,1)} %w_in.1, ...), custom_call_target="tpu_custom_call" | custom-call | tf_op jit(solution)/shard_map/depth_step/pallas_call | solution.py:358
  129.6 1.7 %copy.12 = bf16[16,16,512]{2,1,0:T(8,128)(2,1)} copy(bf16[16,16,512]{2,1,0:T(8,128)(2,1)} %bitcast.2) | data formatting | bytes 524288

commit v3 on v2

--- a/solution.py
+++ b/solution.py
@@ -35,7 +35,7 @@
 
 def kernel(gate_in, up_in, dw_in, res_in, gain, w_in, e_in, q_in, tok, dgain, out,
            gate, up, dw, res, hid, own, a_s, a_r, zs, ys, y_rel, y_r, tf, wbuf, ebuf, qbuf,
-           xb, acc, looked, packed, q_all, qp, rel,
+           xs, acc, looked, packed, q_all, qp, rel,
            in_sem, own_sem, a_ss, a_rs, y_ss, y_rs, b_ss, b_rs, c_ss, c_rs, p_rs,
            d_ss, d_rs, r_ss, r_rs):
     f = lax.axis_index("frames")
@@ -87,6 +87,19 @@
     def _():
         pl.semaphore_signal(sem, inc=1, device_id=inner, device_id_type=MESH)
 
+    for copy in loads:
+        copy.wait()
+    g = gate[...].astype(F32)
+    hid[...] = (g / (1.0 + jnp.exp(-g)) * up[...].astype(F32)).astype(BF16)
+
+    def product(s):
+        for d in (0, 1):
+            blk = mod8(z - 1 - s) if d == 0 else mod8(z + 1 + s)
+            cols = pl.ds(pl.multiple_of(blk * 512, 512), 512)
+            own[d] = jnp.dot(hid[d * 128:(d + 1) * 128, :], dw[:, cols],
+                             preferred_element_type=F32).reshape(2, 64, 512)
+
+    product(0)
     pl.semaphore_wait(sem, len(peers) + lax.rem((yl + 1) // 2, 2))
 
     sent = []
@@ -120,6 +133,9 @@
     def c_wait(a, bx, by, half=None):
         c_copy(a, 0, c_slot(a, bx, by, half), bx, by, twin, half).wait_recv()
 
+    def y_next(i):
+        return inner if i == 1 else dev(x, y_hi * 4 + mod4((yl - 1) * 3), z, core)
+
     def c_col(a, i):
         by = order[i]
         src = c_slot(a, x, by)
@@ -127,9 +143,7 @@
         n = 5 + (i - 1) * 4
         for d in (0, 1):
             go(c_copy(a, n + d, src, x, by, xn[d]))
-        target = dev(x, y_hi * 4 + (3 - yl), z, core) if i == 1 else dev(
-            x, y_hi * 4 + mod4((yl - 1) * 3), z, core)
-        c_go_mid(c_copy(a, n + 2, src, x, by, target))
+        c_go_mid(c_copy(a, n + 2, src, x, by, y_next(i)))
         go(c_twin(a, n + 3, src, x, by))
 
     def c_row(a, i):
@@ -148,9 +162,37 @@
             c_wait(a, bx, by, half)
         go(c_twin(a, 33 + i, c_slot(a, bx, by), bx, by))
 
-    def c_done(a):
-        places[a].wait()
-        for bx in range(4):
+    def e_spread(n, bx):
+        src = c_slot(1, bx, yl)
+        go(c_copy(1, n, src, bx, yl, near))
+        c_go_mid(c_copy(1, n + 1, src, bx, yl, inner))
+        go(c_twin(1, n + 2, src, bx, yl))
+
+    def e_row():
+        for d in (0, 1):
+            bx = mod4(x - 1) if d == 0 else mod4(x + 1)
+            c_wait(1, bx, yl)
+            go(c_copy(1, 5 + d, c_slot(1, bx, yl, d), bx, yl, xn[d], d))
+            e_spread(7 + 3 * d, bx)
+
+    def e_far():
+        bx = mod4(x + 2)
+        for half in (0, 1):
+            c_wait(1, bx, yl, half)
+        e_spread(13, bx)
+
+    def e_col(i):
+        by = order[i]
+        for k, step in enumerate((0, 1, 3, 2)):
+            bx = mod4(x + step)
+            src = c_slot(1, bx, by)
+            c_wait(1, bx, by)
+            n = 16 + (i - 1) * 8 + 2 * k
+            c_go_mid(c_copy(1, n, src, bx, by, y_next(i)))
+            go(c_twin(1, n + 1, src, bx, by))
+
+    def c_done(a, columns):
+        for bx in columns:
             for by in range(4):
                 slot = c_slot(a, bx, by, None, 1 - core)
                 send(slot, slot, c_ss.at[a, 0], p_rs.at[a, bx, by], twin).wait_recv()
@@ -164,36 +206,32 @@
     def y_copy2(d, u):
         return send(y_rel.at[d, u], y_r.at[d, u], y_ss.at[1, d, u], y_rs.at[1, d, u], yn[d])
 
-    c_own(0)
-    for copy in loads:
-        copy.wait()
-    g = gate[...].astype(F32)
-    hid[...] = (g / (1.0 + jnp.exp(-g)) * up[...].astype(F32)).astype(BF16)
+    for a in range(3):
+        c_own(a)
 
     def after_a(s):
-        if s == 1:
+        if s == 2:
+            c_row(0, 0)
             c_col(0, 1)
-            c_row(0, 0)
+            e_row()
         if s == 3:
+            c_row(2, 0)
+            c_col(2, 1)
+            e_far()
+        if s == 5:
             c_col(0, 2)
             c_row(0, 1)
+        if s == 6:
+            c_col(2, 2)
             c_far(0, 0)
-        if s == 5:
-            c_col(0, 3)
-            c_row(0, 2)
-            c_far(0, 1)
-            c_own(1)
-            c_own(2)
+            c_far(2, 0)
         if s == 7:
-            c_row(0, 3)
-            c_far(0, 2)
+            c_row(2, 1)
+            e_col(1)
 
     for s in range(8):
-        for d in (0, 1):
-            blk = mod8(z - 1 - s) if d == 0 else mod8(z + 1 + s)
-            cols = pl.ds(pl.multiple_of(blk * 512, 512), 512)
-            own[d] = jnp.dot(hid[d * 128:(d + 1) * 128, :], dw[:, cols],
-                             preferred_element_type=F32).reshape(2, 64, 512)
+        if s:
+            product(s)
         for u in (0, 1):
             for d in (0, 1):
                 val = own[d, u]
@@ -216,30 +254,39 @@
         for d in (0, 1):
             y_copy(d, u).wait_recv()
             go(y_copy2(d, u))
-        if u == 0:
-            c_far(0, 3)
-            for a in (1, 2):
-                c_col(a, 1)
-                c_row(a, 0)
+    c_col(0, 3)
+    c_col(2, 3)
+    c_row(0, 2)
 
     def b_copy(d, s, h):
         blk = mod8(z - s) if d == 0 else mod8(z + s)
         ref = tf.at[blk, h]
         return send(ref, ref, b_ss.at[d, s, h], b_rs.at[d, s, h], zn[d])
 
-    def block(i):
+    def scaled(i):
         v = tf[i].reshape(256, 512).astype(F32)
         cols = pl.ds(pl.multiple_of(i * 512, 512), 512)
-        xb[...] = (v * gain[:, cols].astype(F32)).astype(BF16)
+        xs[:, cols] = (v * gain[:, cols].astype(F32)).astype(BF16)
+        return jnp.sum(v * v, axis=-1, keepdims=True)
+
+    def project(bx, first):
+        depth = pl.ds(pl.multiple_of(bx * 1024, 1024), 1024)
 
         def tile(n, carry):
             cols = pl.ds(pl.multiple_of(n * 256, 256), 256)
-            rows = pl.ds(pl.multiple_of(i * 512, 512), 512)
-            acc[:, cols] += jnp.dot(xb[...], wbuf[rows, cols], preferred_element_type=F32)
+            part = jnp.dot(xs[:, depth], wbuf[depth, cols], preferred_element_type=F32)
+            acc[:, cols] = part if first else acc[:, cols] + part
             return carry
 
         lax.fori_loop(0, 4, tile, 0)
-        return jnp.sum(v * v, axis=-1, keepdims=True)
+
+    def look_up(bx, first):
+        depth = pl.ds(pl.multiple_of(bx * 256, 256), 256)
+        rows = lax.broadcasted_iota(jnp.int32, (256, 256), 0) + bx * 256
+        matches = jnp.where(tok[...] == rows, 1.0, 0.0).astype(BF16)
+        part = lax.dot_general(matches, ebuf[depth], (((0,), (0,)), ((), ())),
+                               preferred_element_type=F32)
+        looked[...] = part if first else looked[...] + part
 
     for d in (0, 1):
         for u in (0, 1):
@@ -247,12 +294,10 @@
             tf[z, d, u * 64:(u + 1) * 64, :] = (zs[d, u] + y_r[d, u].astype(F32)).astype(BF16)
         for way in (0, 1):
             go(b_copy(way, 0, d))
-    acc[...] = jnp.zeros_like(acc)
-    for a in (1, 2):
-        c_col(a, 2)
-        c_row(a, 1)
-        c_far(a, 0)
-    total = jnp.zeros((256, 1), F32)
+    e_col(2)
+    c_far(0, 1)
+    c_far(2, 1)
+    total = scaled(z)
     for s in range(1, 5):
         for h in (0, 1):
             for d in (0, 1):
@@ -262,28 +307,29 @@
                 if s < 3 or (s == 3 and h == d):
                     go(b_copy(d, s, h))
         if s == 1:
-            for a in (1, 2):
-                c_col(a, 3)
-                c_row(a, 2)
-                c_far(a, 1)
-            c_done(0)
-            total = total + block(z)
+            c_row(2, 2)
+            e_col(3)
         if s == 2:
-            for a in (1, 2):
-                c_row(a, 3)
-                c_far(a, 2)
-        total = total + block(mod8(z - s))
+            c_row(0, 3)
+        if s == 3:
+            c_far(0, 2)
+            c_far(2, 2)
+        total = total + scaled(mod8(z - s))
         if s < 4:
-            total = total + block(mod8(z + s))
-        if s == 3:
-            for a in (1, 2):
-                c_far(a, 3)
-            c_done(1)
-            rows = lax.broadcasted_iota(jnp.int32, (1024, 256), 0)
-            matches = jnp.where(tok[...] == rows, 1.0, 0.0).astype(BF16)
-            looked[...] = lax.dot_general(matches, ebuf[...], (((0,), (0,)), ((), ())),
-                                          preferred_element_type=F32)
-            c_done(2)
+            total = total + scaled(mod8(z + s))
+    c_row(2, 3)
+    for copy in places:
+        copy.wait()
+    ring = (x, mod4(x + 1), mod4(x + 3), mod4(x + 2))
+    c_done(1, range(4))
+    for i in range(4):
+        if i == 3:
+            c_far(0, 3)
+            c_far(2, 3)
+        c_done(0, ring[i:i + 1])
+        project(ring[i], i == 0)
+        look_up(ring[i], i == 0)
+    c_done(2, range(4))
 
     scale = lax.rsqrt(total * (1.0 / 4096) + 1e-05)
     depth = (acc[...] * scale + looked[...]).astype(BF16).astype(F32)
@@ -378,7 +424,7 @@
             pltpu.VMEM((4096, 1024), BF16),
             pltpu.VMEM((1024, 1024), BF16),
             pltpu.VMEM((1024, 3 * WIDTH), BF16),
-            pltpu.VMEM((256, 512), BF16),
+            pltpu.VMEM((256, 4096), BF16),
             pltpu.VMEM((256, 1024), F32),
             pltpu.VMEM((256, 1024), F32),
             pltpu.VMEM((256, 3 * WIDTH), BF16),

time: 131 us -> 139 us (1.061)
  the two profiles are of different devices: /device:TPU:87 before, /device:TPU:1 now
where the time goes in v3:
time: 139 us
  Pallas kernels  136 us (98%)
  local copies, waits for them, and re-layouts  2.98 us (2%)
    pallas_call x1, Pallas kernels, per_device(): pl.pallas_call(kernel, name='depth_step', out_shape=jax.ShapeDtypeStruct(...  136 us

profile of v3, /device:TPU:1, one launch (start us, length us, event | category | flops | bytes accessed | tf_op | source)
XLA Modules:
  0.0 139.2 jit_solution(15981408351685618796)
XLA Ops:
  0.0 1.3 reshape.9.gain
  1.3 136.2 %depth_step.1 = bf16[256,512]{1,0:T(8,128)(2,1)} custom-call(bf16[256,384]{1,0:T(8,128)(2,1)} %gate_in.1, bf16[256,384]{1,0:T(8,128)(2,1)} %up_in.1, bf16[384,4096]{1,0:T(8,128)(2,1)} %dw_in.1, bf16[256,256]{1,0:T(8,128)(2,1)} %res_in.1, bf16[1,4096]{1,0:T(2,128)(2,1)} %reshape.9.gain, bf16[1,128,1024]{2,1,0:T(8,128)(2,1)} %w_in.1, ...), custom_call_target="tpu_custom_call" | custom-call | tf_op jit(solution)/shard_map/depth_step/pallas_call | solution.py:404
  137.5 1.7 %copy.12 = bf16[16,16,512]{2,1,0:T(8,128)(2,1)} copy(bf16[16,16,512]{2,1,0:T(8,128)(2,1)} %bitcast.2) | data formatting | bytes 524288

commit v4 on v3

--- a/solution.py
+++ b/solution.py
@@ -12,6 +12,28 @@
 F32 = jnp.float32
 BF16 = jnp.bfloat16
 SHARD_ROWS = (128, 32, 32)
+PLAN = {
+    "start": (("own", 0), ("own", 2), ("cy", 0),),
+    "A0": (("cy", 1), ("cy", 2),),
+    "A3": (("col", 1, 1), ("col", 0, 1), ("row", 0, 0), ("col", 0, 2),),
+    "A4": (("col", 1, 2),),
+    "A5": (("col", 2, 2), ("col", 2, 1),),
+    "A6": (("row", 0, 1), ("col", 1, 3),),
+    "A7": (("own", 1), ("col", 0, 3),),
+    "Y0": (("row", 2, 0),),
+    "Y1": (("row", 1, 1),),
+    "B0": (("row", 1, 0),),
+    "B1": (("row", 0, 2), ("far", 0, 0),),
+    "B2": (("row", 1, 2), ("row", 0, 3),),
+    "B2a": (("far", 1, 0), ("far", 1, 1), ("far", 2, 0),),
+    "B3": (("col", 2, 3), ("row", 1, 3),),
+    "C1": (("row", 2, 2), ("far", 0, 1),),
+    "B4": (("far", 0, 2),),
+    "C2": (("row", 2, 3), ("far", 0, 3), ("far", 1, 2), ("far", 2, 2),),
+    "C3": (("far", 1, 3),),
+    "P0": (("row", 2, 1), ("far", 2, 3),),
+    "P3": (("far", 2, 1),),
+}
 
 
 def dev(x, y, z, core):
@@ -34,9 +56,9 @@
 
 
 def kernel(gate_in, up_in, dw_in, res_in, gain, w_in, e_in, q_in, tok, dgain, out,
-           gate, up, dw, res, hid, own, a_s, a_r, zs, ys, y_rel, y_r, tf, wbuf, ebuf, qbuf,
-           xs, acc, looked, packed, q_all, qp, rel,
-           in_sem, own_sem, a_ss, a_rs, y_ss, y_rs, b_ss, b_rs, c_ss, c_rs, p_rs,
+           gate, up, dw, res, hid, own, a_s, a_r, zs, ys, y_rel, y_r, t_rel, tf, wbuf, ebuf, qbuf,
+           gains, xs, acc, looked, packed, q_all, qp, rel,
+           in_sem, own_sem, a_ss, a_rs, y_ss, y_rs, t_ss, t_rs, b_ss, b_rs, c_ss, c_rs, p_rs,
            d_ss, d_rs, r_ss, r_rs):
     f = lax.axis_index("frames")
     b = lax.axis_index("book")
@@ -99,6 +121,7 @@
             own[d] = jnp.dot(hid[d * 128:(d + 1) * 128, :], dw[:, cols],
                              preferred_element_type=F32).reshape(2, 64, 512)
 
+    gains[...] = gain[...].astype(F32)
     product(0)
     pl.semaphore_wait(sem, len(peers) + lax.rem((yl + 1) // 2, 2))
 
@@ -115,6 +138,12 @@
 
     def c_twin(a, n, src, bx, by):
         return send(src, c_slot(a, bx, by), c_ss.at[a, n], p_rs.at[a, bx, by], twin)
+
+    def c_own(a):
+        src = shards[a].at[0]
+        for d in (0, 1):
+            go(c_copy(a, d, src, x, yl, xn[d]))
+        go(c_twin(a, 4, src, x, yl))
 
     def c_go_mid(copy):
         @pl.when(mid)
@@ -122,19 +151,16 @@
             copy.start()
         sent_mid.append(copy)
 
-    def c_own(a):
+    def y_next(i):
+        return inner if i == 1 else dev(x, y_hi * 4 + mod4((yl - 1) * 3), z, core)
+
+    def c_along_y(a):
         src = shards[a].at[0]
-        for d in (0, 1):
-            go(c_copy(a, d, src, x, yl, xn[d]))
         go(c_copy(a, 2, src, x, yl, near))
         c_go_mid(c_copy(a, 3, src, x, yl, inner))
-        go(c_twin(a, 4, src, x, yl))
 
     def c_wait(a, bx, by, half=None):
         c_copy(a, 0, c_slot(a, bx, by, half), bx, by, twin, half).wait_recv()
-
-    def y_next(i):
-        return inner if i == 1 else dev(x, y_hi * 4 + mod4((yl - 1) * 3), z, core)
 
     def c_col(a, i):
         by = order[i]
@@ -162,34 +188,11 @@
             c_wait(a, bx, by, half)
         go(c_twin(a, 33 + i, c_slot(a, bx, by), bx, by))
 
-    def e_spread(n, bx):
-        src = c_slot(1, bx, yl)
-        go(c_copy(1, n, src, bx, yl, near))
-        c_go_mid(c_copy(1, n + 1, src, bx, yl, inner))
-        go(c_twin(1, n + 2, src, bx, yl))
-
-    def e_row():
-        for d in (0, 1):
-            bx = mod4(x - 1) if d == 0 else mod4(x + 1)
-            c_wait(1, bx, yl)
-            go(c_copy(1, 5 + d, c_slot(1, bx, yl, d), bx, yl, xn[d], d))
-            e_spread(7 + 3 * d, bx)
-
-    def e_far():
-        bx = mod4(x + 2)
-        for half in (0, 1):
-            c_wait(1, bx, yl, half)
-        e_spread(13, bx)
-
-    def e_col(i):
-        by = order[i]
-        for k, step in enumerate((0, 1, 3, 2)):
-            bx = mod4(x + step)
-            src = c_slot(1, bx, by)
-            c_wait(1, bx, by)
-            n = 16 + (i - 1) * 8 + 2 * k
-            c_go_mid(c_copy(1, n, src, bx, by, y_next(i)))
-            go(c_twin(1, n + 1, src, bx, by))
+    stages = {"own": c_own, "cy": c_along_y, "col": c_col, "row": c_row, "far": c_far}
+
+    def pass_on(place):
+        for stage, *which in PLAN.get(place, ()):
+            stages[stage](*which)
 
     def c_done(a, columns):
         for bx in columns:
@@ -206,29 +209,7 @@
     def y_copy2(d, u):
         return send(y_rel.at[d, u], y_r.at[d, u], y_ss.at[1, d, u], y_rs.at[1, d, u], yn[d])
 
-    for a in range(3):
-        c_own(a)
-
-    def after_a(s):
-        if s == 2:
-            c_row(0, 0)
-            c_col(0, 1)
-            e_row()
-        if s == 3:
-            c_row(2, 0)
-            c_col(2, 1)
-            e_far()
-        if s == 5:
-            c_col(0, 2)
-            c_row(0, 1)
-        if s == 6:
-            c_col(2, 2)
-            c_far(0, 0)
-            c_far(2, 0)
-        if s == 7:
-            c_row(2, 1)
-            e_col(1)
-
+    pass_on("start")
     for s in range(8):
         if s:
             product(s)
@@ -243,30 +224,36 @@
                     go(a_copy(d, u, s))
                 else:
                     zs[d, u] = val
-                    cols = pl.ds(pl.multiple_of(y_hi * 256, 256), 256)
-                    rows = pl.ds(d * 128 + u * 64, 64)
-                    zs[d, u, :, cols] = zs[d, u, :, cols] + res[rows, :].astype(F32)
-                    ys[d, u] = zs[d, u].astype(BF16)
+                    cols = pl.ds(pl.multiple_of((1 - y_hi) * 256, 256), 256)
+                    ys[d, u] = zs[d, u, :, cols].astype(BF16)
                     go(y_copy(d, u))
-        after_a(s)
+        pass_on("A%d" % s)
 
     for u in (0, 1):
         for d in (0, 1):
             y_copy(d, u).wait_recv()
             go(y_copy2(d, u))
-    c_col(0, 3)
-    c_col(2, 3)
-    c_row(0, 2)
-
-    def b_copy(d, s, h):
-        blk = mod8(z - s) if d == 0 else mod8(z + s)
+        pass_on("Y%d" % u)
+
+    planes = (y_hi, 1 - y_hi)
+
+    def b_copy(k, d, s, h):
+        blk = (mod8(z - s) if d == 0 else mod8(z + s)) * 2 + planes[k]
         ref = tf.at[blk, h]
-        return send(ref, ref, b_ss.at[d, s, h], b_rs.at[d, s, h], zn[d])
+        return send(ref, ref, b_ss.at[k, d, s, h], b_rs.at[k, d, s, h], zn[d])
+
+    def t_copy(d):
+        return send(tf.at[b, d], t_rel.at[d], t_ss.at[0, d], t_rs.at[0, d], yn[d])
+
+    def t_copy2(d):
+        source = (way_down, way_up)[d] // 4
+        return send(t_rel.at[d], tf.at[z * 2 + source, d], t_ss.at[1, d], t_rs.at[1, d], yn[d])
 
     def scaled(i):
-        v = tf[i].reshape(256, 512).astype(F32)
-        cols = pl.ds(pl.multiple_of(i * 512, 512), 512)
-        xs[:, cols] = (v * gain[:, cols].astype(F32)).astype(BF16)
+        v = tf[i].reshape(256, 256).astype(F32)
+        for j in (0, 1):
+            cols = pl.ds(pl.multiple_of(i * 256 + j * 128, 128), 128)
+            xs[:, cols] = (v[:, j * 128:(j + 1) * 128] * gains[pl.ds(i * 2 + j, 1), :]).astype(BF16)
         return jnp.sum(v * v, axis=-1, keepdims=True)
 
     def project(bx, first):
@@ -288,98 +275,131 @@
                                preferred_element_type=F32)
         looked[...] = part if first else looked[...] + part
 
-    for d in (0, 1):
-        for u in (0, 1):
-            y_copy2(d, u).wait_recv()
-            tf[z, d, u * 64:(u + 1) * 64, :] = (zs[d, u] + y_r[d, u].astype(F32)).astype(BF16)
-        for way in (0, 1):
-            go(b_copy(way, 0, d))
-    e_col(2)
-    c_far(0, 1)
-    c_far(2, 1)
-    total = scaled(z)
-    for s in range(1, 5):
+    def b_step(k, s):
         for h in (0, 1):
             for d in (0, 1):
                 if s == 4 and h != d:
                     continue
-                b_copy(d, s - 1, h).wait_recv()
+                b_copy(k, d, s - 1, h).wait_recv()
                 if s < 3 or (s == 3 and h == d):
-                    go(b_copy(d, s, h))
-        if s == 1:
-            c_row(2, 2)
-            e_col(3)
-        if s == 2:
-            c_row(0, 3)
-        if s == 3:
-            c_far(0, 2)
-            c_far(2, 2)
-        total = total + scaled(mod8(z - s))
-        if s < 4:
-            total = total + scaled(mod8(z + s))
-    c_row(2, 3)
+                    go(b_copy(k, d, s, h))
+
+    def scaled_pair(k, s):
+        part = scaled(mod8(z - s) * 2 + planes[k])
+        if 0 < s < 4:
+            part = part + scaled(mod8(z + s) * 2 + planes[k])
+        return part
+
+    mine = pl.ds(pl.multiple_of(y_hi * 256, 256), 256)
+    for d in (0, 1):
+        for u in (0, 1):
+            y_copy2(d, u).wait_recv()
+            rows = pl.ds(d * 128 + u * 64, 64)
+            whole = zs[d, u, :, mine] + y_r[d, u].astype(F32) + res[rows, :].astype(F32)
+            tf[b, d, u * 64:(u + 1) * 64, :] = whole.astype(BF16)
+        for way in (0, 1):
+            go(b_copy(0, way, 0, d))
+        go(t_copy(d))
+    pass_on("B0")
+    total = scaled_pair(0, 0)
+    b_step(0, 1)
+    pass_on("B1")
+    for d in (0, 1):
+        t_copy(d).wait_recv()
+        go(t_copy2(d))
+    pass_on("B1a")
+    total = total + scaled_pair(0, 1)
+    b_step(0, 2)
+    pass_on("B2")
+    total = total + scaled_pair(0, 2)
+    for d in (0, 1):
+        t_copy2(d).wait_recv()
+        for way in (0, 1):
+            go(b_copy(1, way, 0, d))
+    pass_on("B2a")
+    b_step(0, 3)
+    pass_on("B3")
+    total = total + scaled_pair(0, 3) + scaled_pair(1, 0)
+    b_step(1, 1)
+    pass_on("C1")
+    total = total + scaled_pair(1, 1)
+    b_step(0, 4)
+    pass_on("B4")
+    total = total + scaled_pair(0, 4)
+    b_step(1, 2)
+    pass_on("C2")
+    total = total + scaled_pair(1, 2)
+    b_step(1, 3)
+    pass_on("C3")
+    total = total + scaled_pair(1, 3)
+    b_step(1, 4)
+    total = total + scaled_pair(1, 4)
     for copy in places:
         copy.wait()
     ring = (x, mod4(x + 1), mod4(x + 3), mod4(x + 2))
-    c_done(1, range(4))
+    pass_on("P0")
     for i in range(4):
         if i == 3:
-            c_far(0, 3)
-            c_far(2, 3)
-        c_done(0, ring[i:i + 1])
+            pass_on("P3")
+        for a in (0, 1):
+            c_done(a, ring[i:i + 1])
         project(ring[i], i == 0)
         look_up(ring[i], i == 0)
+    pass_on("Q")
     c_done(2, range(4))
 
     scale = lax.rsqrt(total * (1.0 / 4096) + 1e-05)
     depth = (acc[...] * scale + looked[...]).astype(BF16).astype(F32)
     moment = jnp.mean(depth * depth, axis=-1, keepdims=True)
     normed = (depth * lax.rsqrt(moment + 1e-05) * dgain[...].astype(F32)).astype(BF16)
-    packed[...] = jnp.dot(normed, qbuf[...], preferred_element_type=F32).astype(BF16)
-
     def rows_of(zz, plane):
         return pl.ds(pl.multiple_of((zz * 2 + plane) * 16, 16), 16)
 
-    def slot(zz, plane):
-        return q_all.at[rows_of(zz, plane)]
-
-    def first(i):
-        return send(packed.at[rows_of(mod8(z + i), 1 - y_hi)], rel.at[i],
-                    r_ss.at[i], r_rs.at[i], yn[i // 4])
-
-    def second(i):
+    def slot(k, zz, plane):
+        return q_all.at[k, rows_of(zz, plane)]
+
+    def first(k, i):
+        return send(packed.at[k, rows_of(mod8(z + i), 1 - y_hi)], rel.at[k, i],
+                    r_ss.at[k, i], r_rs.at[k, i], yn[i // 4])
+
+    def second(k, i):
         source = (way_down, way_up)[i // 4] // 4
-        return send(rel.at[i], slot(z, source), d_ss.at[8 + i], d_rs.at[8 + i],
+        return send(rel.at[k, i], slot(k, z, source), d_ss.at[k, 8 + i], d_rs.at[k, 8 + i],
                     dev(x, (way_up, way_down)[i // 4], mod8(z + i), core))
 
-    def direct(i):
-        return send(packed.at[rows_of(mod8(z + i), y_hi)], slot(z, y_hi),
-                    d_ss.at[i], d_rs.at[i], dev(x, y, mod8(z + i), core))
-
-    for i in (3, 4, 2, 5, 1, 6, 0, 7):
-        go(first(i))
-    for i in (4, 3, 5, 2, 6, 1, 7):
-        go(direct(i))
-    q_all[rows_of(z, y_hi), :] = packed[rows_of(z, y_hi), :]
-    for i in (3, 4, 2, 5, 1, 6, 0, 7):
-        first(i).wait_recv()
-        go(second(i))
-    for i in range(1, 8):
-        direct(i).wait_recv()
-    for i in range(8):
-        second(i).wait_recv()
+    def direct(k, i):
+        return send(packed.at[k, rows_of(mod8(z + i), y_hi)], slot(k, z, y_hi),
+                    d_ss.at[k, i], d_rs.at[k, i], dev(x, y, mod8(z + i), core))
+
+    for k in range(3):
+        packed[k] = jnp.dot(normed, qbuf[:, k * WIDTH:(k + 1) * WIDTH],
+                            preferred_element_type=F32).astype(BF16)
+        for i in (3, 4, 2, 5, 1, 6, 0, 7):
+            go(first(k, i))
+        for i in (4, 3, 5, 2, 6, 1, 7):
+            go(direct(k, i))
+        q_all[k, rows_of(z, y_hi), :] = packed[k, rows_of(z, y_hi), :]
+    for k in range(3):
+        for i in (3, 4, 2, 5, 1, 6, 0, 7):
+            first(k, i).wait_recv()
+            go(second(k, i))
+    for k in range(3):
+        for i in range(1, 8):
+            direct(k, i).wait_recv()
+        for i in range(8):
+            second(k, i).wait_recv()
 
     row = lax.broadcasted_iota(jnp.int32, (256, 256), 0)
     col = lax.broadcasted_iota(jnp.int32, (256, 256), 1)
     same = lax.rem(col, 16) == row // 16
     swap = jnp.where(same & (col // 16 == lax.rem(row, 16)), HD ** -0.5, 0.0).astype(BF16)
     seen = same & (col // 16 <= lax.rem(row, 16))
-    qp[...] = jnp.dot(swap, q_all[:, :WIDTH], preferred_element_type=F32).astype(BF16)
+    qp[...] = jnp.dot(swap, q_all[0], preferred_element_type=F32).astype(BF16)
     for h in range(0, H, 2):
         pair = []
         for k in (h, h + 1):
-            keys = q_all[:, WIDTH + k * HD:WIDTH + (k + 1) * HD]
-            values = q_all[:, 2 * WIDTH + k * HD:2 * WIDTH + (k + 1) * HD]
+            keys = q_all[1, :, k * HD:(k + 1) * HD]
+            values = q_all[2, :, k * HD:(k + 1) * HD]
             scores = lax.dot_general(qp[:, k * HD:(k + 1) * HD], keys, (((1,), (1,)), ((), ())),
                                      preferred_element_type=F32)
             scores = jnp.where(seen, scores, -1e30)
@@ -417,29 +437,32 @@
             pltpu.VMEM((2, 2, 7, 64, 512), BF16),
             pltpu.VMEM((2, 2, 7, 64, 512), BF16),
             pltpu.VMEM((2, 2, 64, 512), F32),
-            pltpu.VMEM((2, 2, 64, 512), BF16),
-            pltpu.VMEM((2, 2, 64, 512), BF16),
-            pltpu.VMEM((2, 2, 64, 512), BF16),
-            pltpu.VMEM((8, 2, 128, 512), BF16),
+            pltpu.VMEM((2, 2, 64, 256), BF16),
+            pltpu.VMEM((2, 2, 64, 256), BF16),
+            pltpu.VMEM((2, 2, 64, 256), BF16),
+            pltpu.VMEM((2, 128, 256), BF16),
+            pltpu.VMEM((16, 2, 128, 256), BF16),
             pltpu.VMEM((4096, 1024), BF16),
             pltpu.VMEM((1024, 1024), BF16),
             pltpu.VMEM((1024, 3 * WIDTH), BF16),
+            pltpu.VMEM((32, 128), F32),
             pltpu.VMEM((256, 4096), BF16),
             pltpu.VMEM((256, 1024), F32),
             pltpu.VMEM((256, 1024), F32),
-            pltpu.VMEM((256, 3 * WIDTH), BF16),
-            pltpu.VMEM((256, 3 * WIDTH), BF16),
+            pltpu.VMEM((3, 256, WIDTH), BF16),
+            pltpu.VMEM((3, 256, WIDTH), BF16),
             pltpu.VMEM((256, WIDTH), BF16),
-            pltpu.VMEM((8, 16, 3 * WIDTH), BF16),
+            pltpu.VMEM((3, 8, 16, WIDTH), BF16),
             dma((4,)), dma((3,)),
             dma((2, 2, 7)), dma((2, 2, 7)),
             dma((2, 2, 2)), dma((2, 2, 2)),
-            dma((2, 4, 2)), dma((2, 4, 2)),
+            dma((2, 2)), dma((2, 2)),
+            dma((2, 2, 4, 2)), dma((2, 2, 4, 2)),
             dma((3, 40)), dma((3, 4, 4, 2)), dma((3, 4, 4)),
-            dma((16,)), dma((16,)), dma((8,)), dma((8,)),
+            dma((3, 16)), dma((3, 16)), dma((3, 8)), dma((3, 8)),
         ],
         compiler_params=pltpu.CompilerParams(collective_id=0, has_side_effects=True),
-    )(gate_pre, up_pre, down_weight, residual, out_gain.reshape(1, 4096), in_proj, embedding,
+    )(gate_pre, up_pre, down_weight, residual, out_gain.reshape(32, 128), in_proj, embedding,
       qkv_weight, token_ids.reshape(1, 256), depth_gain)
     return out.reshape(16, 16, WIDTH)
 

time: 139 us -> 123 us (0.88)
  the two profiles are of different devices: /device:TPU:1 before, /device:TPU:6 now
where the time goes in v4:
time: 123 us; the launch traced here: 122 us
  Pallas kernels  120 us (98%)
  local copies, waits for them, and re-layouts  1.67 us (1%)
    pallas_call x1, Pallas kernels, per_device(): pl.pallas_call(kernel, name='depth_step', out_shape=jax.ShapeDtypeStruct(...  120 us

profile of v4, /device:TPU:6, one launch (start us, length us, event | category | flops | bytes accessed | tf_op | source)
XLA Modules:
  0.0 121.5 jit_solution(16555649898938743660)
XLA Ops:
  0.0 119.8 %depth_step.1 = bf16[256,512]{1,0:T(8,128)(2,1)} custom-call(bf16[256,384]{1,0:T(8,128)(2,1)} %gate_in.1, bf16[256,384]{1,0:T(8,128)(2,1)} %up_in.1, bf16[384,4096]{1,0:T(8,128)(2,1)} %dw_in.1, bf16[256,256]{1,0:T(8,128)(2,1)} %res_in.1, bf16[32,128]{1,0:T(8,128)(2,1)} %bitcast.4, bf16[1,128,1024]{2,1,0:T(8,128)(2,1)} %w_in.1, bf16[1,32,1024]{2,1,0:T(8,128)(2,1)} %e_in.1, ...), custom_call_target="tpu_custom_call" | custom-call | tf_op jit(solution)/shard_map/depth_step/pallas_call | solution.py:424
  119.8 1.7 %copy.12 = bf16[16,16,512]{2,1,0:T(8,128)(2,1)} copy(bf16[16,16,512]{2,1,0:T(8,128)(2,1)} %bitcast.3) | data formatting | bytes 524288
